TPU v7x, 32 devices: a whole 2x2x4 slice. The times are simulated.
32 devices in a mesh: pairs: 8 (over z, y), dom: 4 (over x, core).
Axes of the slice: x: 2, y: 2, z: 4, core: 2. Of those that a mesh axis runs over, the one named last changes fastest.
Arguments:
- amplitude: bfloat16 [64, 384, 384], P('pairs', 'dom'), may hold values from -2 to 2
- integrals: bfloat16 [64, 384, 384], P('pairs', 'dom'), may hold values from -6 to 6
- virtual_energy: float32 [64, 384], P('pairs'), may hold values from 0.2 to 1.5
- occupied_gap: float32 [64], P('pairs'), may hold values from 0.3 to 1.5
- pair_slot: int32 [64], replicated, may hold values from 0 to 63, as said below
- coupling_source: int32 [128], replicated, may hold values from 0 to 63, as said below
- coupling_target: int32 [128], replicated, may hold values from 0 to 63, as said below
- coupling_fock: float32 [128], P(('pairs', 'dom')), may hold values from -3 to 3
- coupling_intersection: bfloat16 [128, 384, 384], P(('pairs', 'dom')), may hold values from -0.3125 to 0.3125
Outputs:
- updated_amplitude: float32 [64, 384, 384], P('pairs', 'dom')
- residual: float32 [64, 384, 384], P('pairs', 'dom')
Inputs may be any that keep to these rules, and one draw needn't show every extreme that they name: A permutation: pair p is stored at position pair_slot[p], which lies on index pair_slot[p] // 8 of pairs. `coupling_target`: coupling c is held by index c // 16 of pairs, and its target pair is stored on that same index; the two couplings that share a source pair on one holder have different targets. `coupling_source`: among the 16 couplings of one holder, every source pair appears in exactly two, and there are 8 distinct source pairs; of the pairs stored on any one index of pairs, a holder uses at most 2 distinct ones as sources, and exactly 2 for some indices on every holder.
All inputs are finite; a program needn't handle non-finite values.
Results may differ from a plain program's by a relative error of at most 0.0024.
Values may be sent and summed in bfloat16 or wider, within the bound.
A program may use at most 128 MiB of HBM per device.

v0:
```python
import jax
import jax.numpy as jnp
from jax import lax
from jax.sharding import PartitionSpec as P

SRC_CAP = 2


def lookup(table, indices):
    places = jnp.arange(table.shape[0], dtype=jnp.int32)
    return jnp.sum(jnp.where(indices[:, None] == places[None, :], table[None, :], 0), axis=1)


def per_device(
    amplitude,
    integrals,
    virtual_energy,
    occupied_gap,
    pair_slot,
    coupling_source,
    coupling_target,
    coupling_fock,
    coupling_intersection,
):
    holders = lax.axis_size("pairs")
    quarters = lax.axis_size("dom")
    own_pair = lax.axis_index("pairs")
    own_quarter = lax.axis_index("dom")
    pair_count, row_count, width = amplitude.shape
    couplings = coupling_source.shape[0] // holders
    quarter_couplings = coupling_intersection.shape[0]
    source_slot = lookup(pair_slot, coupling_source).reshape(holders, couplings)
    target_slot = lookup(pair_slot, coupling_target).reshape(holders, couplings)
    source_owner = source_slot // pair_count
    source_local = source_slot % pair_count
    held_owner = lax.dynamic_index_in_dim(source_owner, own_pair, 0, keepdims=False)
    held_local = lax.dynamic_index_in_dim(source_local, own_pair, 0, keepdims=False)
    held_target = lax.dynamic_index_in_dim(target_slot, own_pair, 0, keepdims=False) % pair_count
    local_numbers = jnp.arange(pair_count, dtype=jnp.int32)
    owner_numbers = jnp.arange(holders, dtype=jnp.int32)
    capacity = SRC_CAP
    wanted = jnp.any(
        (source_owner[:, :, None] == own_pair)
        & (source_local[:, :, None] == local_numbers[None, None, :]),
        axis=1,
    )
    wanted_count = wanted.astype(jnp.int32)
    order = jnp.cumsum(wanted_count, axis=1) - wanted_count
    slot_numbers = jnp.arange(capacity, dtype=jnp.int32)
    chosen = wanted[:, None, :] & (order[:, None, :] == slot_numbers[None, :, None])
    picked = jnp.sum(jnp.where(chosen, local_numbers[None, None, :], 0), axis=2)
    match = (held_owner[:, None, None] == owner_numbers[None, :, None]) & (
        held_local[:, None, None] == local_numbers[None, None, :]
    )
    needed = jnp.any(match, axis=0).astype(jnp.int32)
    held_order = jnp.cumsum(needed, axis=1) - needed
    held_rank = jnp.sum(jnp.where(match, held_order[None], 0), axis=(1, 2))
    held_slot = held_owner * capacity + held_rank
    energy_rows = lax.dynamic_slice_in_dim(virtual_energy, own_quarter * row_count, row_count, 1)
    denominator = energy_rows[:, :, None] + virtual_energy[:, None, :] + occupied_gap[:, None, None]
    target_select = (held_target[None, :] == local_numbers[:, None]).astype(jnp.bfloat16)
    current = amplitude.astype(jnp.float32)
    sent = current.astype(jnp.bfloat16)
    outgoing = jnp.take(sent, picked.reshape(-1), axis=0).reshape(
        holders, capacity, row_count, width
    )
    arrived = lax.all_to_all(outgoing, "pairs", split_axis=0, concat_axis=0, tiled=True)
    held_rows = jnp.take(arrived.reshape(holders * capacity, row_count, width), held_slot, axis=0)
    grouped = held_rows.reshape(quarters, quarter_couplings, row_count, width)
    whole = lax.all_to_all(grouped, "dom", split_axis=0, concat_axis=2, tiled=True).reshape(
        quarter_couplings, quarters * row_count, width
    )
    left = jnp.einsum(
        "cab,cbd->cad", coupling_intersection, whole, preferred_element_type=jnp.float32
    ).astype(jnp.bfloat16)
    projected = jnp.einsum(
        "cad,ced->cae", left, coupling_intersection, preferred_element_type=jnp.float32
    )
    coupled_term = (coupling_fock[:, None, None] * projected).astype(jnp.bfloat16)
    scattered = lax.all_to_all(
        coupled_term.reshape(quarter_couplings, quarters, row_count, width),
        "dom",
        split_axis=1,
        concat_axis=0,
        tiled=True,
    ).reshape(couplings, row_count, width)
    coupled = jnp.einsum(
        "pc,crd->prd", target_select, scattered, preferred_element_type=jnp.float32
    )
    residual = integrals.astype(jnp.float32) + denominator * current - coupled
    current = current - residual / denominator
    return (current, residual)


def solution(mesh):
    in_specs = (
        P("pairs", "dom", None),
        P("pairs", "dom", None),
        P("pairs", None),
        P("pairs"),
        P(),
        P(),
        P(),
        P(("pairs", "dom")),
        P(("pairs", "dom"), None, None),
    )
    out_specs = (P("pairs", "dom", None), P("pairs", "dom", None))
    return jax.shard_map(
        per_device, mesh=mesh, in_specs=in_specs, out_specs=out_specs, check_vma=False
    )
```

profile of v0, /device:TPU:0, one launch (start us, length us, event | category | flops | bytes accessed | tf_op | source)
XLA Modules:
  0.0 88.6 jit_solution(5788474851340077103)
XLA Ops:
  0.7 0.9 select_reduce_fusion.1
  1.6 0.2 fusion.4
  1.9 0.2 reduce_window_sum.18
  2.0 0.2 select_reduce_fusion.2
  2.3 0.1 copy.46
  2.5 1.9 %gather_fusion = bf16[16,96,384]{2,1,0:T(8,128)(2,1)S(1)} fusion(bf16[8,96,384]{2,1,0:T(8,128)(2,1)} %param.9, s32[1024]{0:T(1024)S(1)} %pad_clamp_fusion.1), kind=kCustom, calls=%fused_computation | custom fusion | bytes 2359360 | tf_op jit(solution)/shard_map/jit(_take)/gather | solution.py:64
  4.4 1.2 %broadcast_select_fusion = bf16[8,2,96,384]{3,2,1,0:T(8,128)(2,1)} fusion(bf16[8,2,96,384]{3,2,1,0:T(8,128)(2,1)S(1)} %bitcast.39, pred[8,2]{1,0:T(8,128)(4,1)S(1)} %copy.46), kind=kLoop, calls=%fused_computation.10 | loop fusion | flops 589824 | bytes 2359312 | tf_op jit(solution)/shard_map/jit(_take)/select_n | solution.py:64
  5.6 7.3 %all-to-all-start = ((bf16[8,2,96,384]{3,2,1,0:T(8,128)(2,1)}), bf16[8,2,96,384]{3,2,1,0:T(8,128)(2,1)S(1)}, u32[]{:S(2)}, u32[]{:S(2)}) async-start(bf16[8,2,96,384]{3,2,1,0:T(8,128)(2,1)} %broadcast_select_fusion), calls=%async_computation | async-start | bytes 2359296 | tf_op jit(solution)/shard_map/all_to_all | solution.py:67
  13.0 0.2 and_reduce_fusion
  13.2 0.2 reduce_window_sum.17
  13.4 0.1 fusion.2
  13.6 27.8 %all-to-all-done = bf16[8,2,96,384]{3,2,1,0:T(8,128)(2,1)S(1)} async-done(((bf16[8,2,96,384]{3,2,1,0:T(8,128)(2,1)}), bf16[8,2,96,384]{3,2,1,0:T(8,128)(2,1)S(1)}, u32[]{:S(2)}, u32[]{:S(2)}) %all-to-all-start) | async-done | bytes 1179680 | tf_op jit(solution)/shard_map/all_to_all | solution.py:67
  41.5 0.8 gather_fusion.1
  42.3 0.2 broadcast_select_fusion.1
  42.5 18.4 %all_to_all.35 = bf16[4,4,96,384]{3,2,1,0:T(8,128)(2,1)S(1)} all-to-all(bf16[4,4,96,384]{3,2,1,0:T(8,128)(2,1)S(1)} %broadcast_select_fusion.1), channel_id=1, replica_groups=mesh['pairs'=8,'dom'=4] {'dom'}, dimensions={0} | all-to-all | bytes 2359296 | tf_op jit(solution)/shard_map/all_to_all | solution.py:70
  60.9 0.1 copy.48
  61.0 0.5 copy-done.3
  61.5 1.8 %multiply_convert_fusion = bf16[4,384,384]{2,1,0:T(8,128)(2,1)S(1)} fusion(bf16[4,384,384]{2,1,0:T(8,128)(2,1)S(1)} %copy-done, bf16[4,384,384]{2,1,0:T(8,128)(2,1)S(1)} %bitcast.42, f32[4]{0:T(128)S(1)} %copy-done.3), kind=kOutput, calls=%fused_computation.2 | convolution fusion | flops 907739136 | bytes 3538960 | tf_op jit(solution)/shard_map/cad,ced->cae/dot_general | solution.py:76
  63.4 1.2 %copy.51 = bf16[4,4,96,384]{3,2,0,1:T(8,128)(2,1)} copy(bf16[4,4,96,384]{3,2,1,0:T(8,128)(2,1)S(1)} %bitcast.43) | data formatting | bytes 2359296 | tf_op jit(solution)/shard_map/reshape | solution.py:81
  64.5 3.7 %all-to-all-start.2 = ((bf16[4,4,96,384]{3,2,0,1:T(8,128)(2,1)}), bf16[4,4,96,384]{3,2,0,1:T(8,128)(2,1)S(1)}, u32[]{:S(2)}, u32[]{:S(2)}) async-start(bf16[4,4,96,384]{3,2,0,1:T(8,128)(2,1)} %copy.51), calls=%async_computation.2 | async-start | bytes 2359296 | tf_op jit(solution)/shard_map/all_to_all | solution.py:80
  68.5 15.5 %all-to-all-done.2 = bf16[4,4,96,384]{3,2,0,1:T(8,128)(2,1)S(1)} async-done(((bf16[4,4,96,384]{3,2,0,1:T(8,128)(2,1)}), bf16[4,4,96,384]{3,2,0,1:T(8,128)(2,1)S(1)}, u32[]{:S(2)}, u32[]{:S(2)}) %all-to-all-start.2) | async-done | bytes 1179680 | tf_op jit(solution)/shard_map/all_to_all | solution.py:80
  84.0 2.2 %convert_subtract_fusion = (f32[8,96,384]{2,0,1:T(8,128)S(1)}, f32[8,96,384]{2,0,1:T(8,128)S(1)}) fusion(f32[8]{0:T(128)S(1)} %copy-done.4, f32[8,384]{1,0:T(8,128)S(1)} %copy-done.2, f32[8,96]{0,1:T(8,128)S(1)} %copy.45, bf16[8,96,384]{2,1,0:T(8,128)(2,1)S(1)} %copy-done.1, bf16[16,96,384]{2,1,0:T(8,128)(2,1)S(1)} %bitcast.41, s32[16]{0:T(128)S(1)} %fusion.12, ...), kind=kOutput, calls=%fused_computation.4 | convolution fusion | flops 12091520 | bytes 4734048 | tf_op jit(solution)/shard_map/pc,crd->prd/dot_general | solution.py:87
  86.2 1.2 %copy.53 = f32[8,96,384]{2,1,0:T(8,128)} copy(f32[8,96,384]{2,0,1:T(8,128)S(1)} %get-tuple-element.18) | data formatting | bytes 2359296
  87.4 1.2 %copy.54 = f32[8,96,384]{2,1,0:T(8,128)} copy(f32[8,96,384]{2,0,1:T(8,128)S(1)} %get-tuple-element.19) | data formatting | bytes 2359296
  (33 shorter events, 0.8 us)
Async XLA Ops:
  0.6 60.4 %copy-start = (bf16[4,384,384]{2,1,0:T(8,128)(2,1)S(1)}, bf16[4,384,384]{2,1,0:T(8,128)(2,1)}, u32[]{:S(2)}) copy-start(bf16[4,384,384]{2,1,0:T(8,128)(2,1)} %param.17) | copy-start | bytes 3538948
  5.6 35.9 %all-to-all-start = ((bf16[8,2,96,384]{3,2,1,0:T(8,128)(2,1)}), bf16[8,2,96,384]{3,2,1,0:T(8,128)(2,1)S(1)}, u32[]{:S(2)}, u32[]{:S(2)}) async-start(bf16[8,2,96,384]{3,2,1,0:T(8,128)(2,1)} %broadcast_select_fusion), calls=%async_computation | async-start | bytes 2359296 | tf_op jit(solution)/shard_map/all_to_all | solution.py:67
  60.9 0.7 copy-start.3
  64.5 3.8 %copy-start.2 = (f32[8,384]{1,0:T(8,128)S(1)}, f32[8,384]{1,0:T(8,128)}, u32[]{:S(2)}) copy-start(f32[8,384]{1,0:T(8,128)} %param.11) | copy-start | bytes 36868
  64.5 19.5 %copy-start.1 = (bf16[8,96,384]{2,1,0:T(8,128)(2,1)S(1)}, bf16[8,96,384]{2,1,0:T(8,128)(2,1)}, u32[]{:S(2)}) copy-start(bf16[8,96,384]{2,1,0:T(8,128)(2,1)} %param.9) | copy-start | bytes 1769476
  64.5 19.5 %copy-start.4 = (f32[8]{0:T(128)S(1)}, f32[8]{0:T(128)}, u32[]{:S(2)}) copy-start(f32[8]{0:T(128)} %param.12) | copy-start | bytes 100
  64.5 19.5 %all-to-all-start.2 = ((bf16[4,4,96,384]{3,2,0,1:T(8,128)(2,1)}), bf16[4,4,96,384]{3,2,0,1:T(8,128)(2,1)S(1)}, u32[]{:S(2)}, u32[]{:S(2)}) async-start(bf16[4,4,96,384]{3,2,0,1:T(8,128)(2,1)} %copy.51), calls=%async_computation.2 | async-start | bytes 2359296 | tf_op jit(solution)/shard_map/all_to_all | solution.py:80
where the time goes:
time: 89 us; the launch traced here: 88.6 us
  waiting for transfers between devices  43.4 us (49%)
  blocking collectives  18.4 us (21%)
  starting transfers between devices  11 us (12%)
  local copies, waits for them, and re-layouts  7.69 us (9%)
  matrix products  3.99 us (4%)
  other arithmetic  3.46 us (4%)
    all_to_all x1, waiting for transfers between devices, per_device(): lax.all_to_all(outgoing, 'pairs', split_axis=0, concat_axis=0, tiled=True)  27.8 us
    all_to_all x1, blocking collectives, per_device(): lax.all_to_all(grouped, 'dom', split_axis=0, concat_axis=2, tiled=True)  18.4 us
    all_to_all x1, waiting for transfers between devices, per_device(): lax.all_to_all(coupled_term.reshape(quarter_couplings, quarters, row_coun...  15.5 us
    all_to_all x1, starting transfers between devices, per_device(): lax.all_to_all(outgoing, 'pairs', split_axis=0, concat_axis=0, tiled=True)  7.31 us
    all_to_all x1, starting transfers between devices, per_device(): lax.all_to_all(coupled_term.reshape(quarter_couplings, quarters, row_coun...  3.66 us
    unnamed x12, local copies, waits for them, and re-layouts  2.97 us
    dot_general x1, matrix products, per_device(): jnp.einsum('pc,crd->prd', target_select, scattered, preferred_element_typ...  2.16 us
    gather x1, local copies, waits for them, and re-layouts, per_device(): jnp.take(sent, picked.reshape(-1), axis=0)  1.87 us
  transfers between devices with their start and end apart: 2, of which 2 were waited for; matrix products, arithmetic and copies ran while one was open for 1% of the time, Pallas kernels for 0%

commit v1 on v0

--- a/solution.py
+++ b/solution.py
@@ -4,6 +4,22 @@
 from jax.sharding import PartitionSpec as P
 
 SRC_CAP = 2
+
+
+def sample_enter(body, join_dim, vector):
+    side_arr = body.shape
+    k_now = body.reshape(
+        *side_arr[:join_dim], vector, side_arr[join_dim] // vector, *side_arr[join_dim + 1 :]
+    )
+    return jnp.moveaxis(k_now, join_dim, 0)
+
+
+def lift_the_domain(buf, pos_dim):
+    buf = jnp.moveaxis(buf, 0, pos_dim)
+    taken_in = buf.shape
+    return buf.reshape(
+        *taken_in[:pos_dim], taken_in[pos_dim] * taken_in[pos_dim + 1], *taken_in[pos_dim + 2 :]
+    )
 
 
 def lookup(table, indices):
@@ -64,7 +80,16 @@
     outgoing = jnp.take(sent, picked.reshape(-1), axis=0).reshape(
         holders, capacity, row_count, width
     )
-    arrived = lax.all_to_all(outgoing, "pairs", split_axis=0, concat_axis=0, tiled=True)
+    outer = lax.axis_size("pairs")
+    reply = lax.axis_index("pairs")
+    inter, y = (outer, reply)
+    val2 = sample_enter(outgoing, 0, inter)
+    history = [val2[y]]
+    for b in range(1, inter):
+        val = val2[y ^ b]
+        history.append(lax.ppermute(val, "pairs", [(ii, ii ^ b) for ii in range(inter)]))
+    val2 = jnp.stack(history)[y ^ jnp.arange(inter)]
+    arrived = lift_the_domain(val2, 0)
     held_rows = jnp.take(arrived.reshape(holders * capacity, row_count, width), held_slot, axis=0)
     grouped = held_rows.reshape(quarters, quarter_couplings, row_count, width)
     whole = lax.all_to_all(grouped, "dom", split_axis=0, concat_axis=2, tiled=True).reshape(

time: 89 us -> 90.6 us (1.018)
  waiting for transfers between devices: 43.4 us -> 30.4 us
  starting transfers between devices: 11 us -> 21.2 us
  local copies, waits for them, and re-layouts: 7.69 us -> 12.5 us
    all_to_all x1 -> x0, waiting for transfers between devices: 27.8 us -> none  [per_device(): lax.all_to_all(outgoing, 'pairs', split_axis=0, concat_axis=0, tiled=True)]
    ppermute x0 -> x7, starting transfers between devices: none -> 17.5 us  [per_device(): lax.ppermute(val, 'pairs', [(ii, ii ^ b) for ii in range(inter)])]
    ppermute x0 -> x7, waiting for transfers between devices: none -> 14.9 us  [per_device(): lax.ppermute(val, 'pairs', [(ii, ii ^ b) for ii in range(inter)])]
    all_to_all x1 -> x0, starting transfers between devices: 7.31 us -> none  [per_device(): lax.all_to_all(outgoing, 'pairs', split_axis=0, concat_axis=0, tiled=True)]
    unnamed x12 -> x20, local copies, waits for them, and re-layouts: 2.97 us -> 6.77 us
    select_n x2, other arithmetic: 1.22 us -> 0.21 us  [per_device(): jnp.take(sent, picked.reshape(-1), axis=0)]
  transfers between devices with their start and end apart: 2 -> 8, of which waited for: 2 -> 4; matrix products, arithmetic and copies ran while one was open for 1% -> 5% of each run, Pallas kernels for 0% -> 0%
where the time goes in v1:
time: 90.6 us; the launch traced here: 90.2 us
  waiting for transfers between devices  30.4 us (34%)
  starting transfers between devices  21.2 us (23%)
  blocking collectives  18.4 us (20%)
  local copies, waits for them, and re-layouts  12.5 us (14%)
  matrix products  3.78 us (4%)
  other arithmetic  2.96 us (3%)
  between operations  0.94 us (1%)
    all_to_all x1, blocking collectives, per_device(): lax.all_to_all(grouped, 'dom', split_axis=0, concat_axis=2, tiled=True)  18.4 us
    ppermute x7, starting transfers between devices, per_device(): lax.ppermute(val, 'pairs', [(ii, ii ^ b) for ii in range(inter)])  17.5 us
    all_to_all x1, waiting for transfers between devices, per_device(): lax.all_to_all(coupled_term.reshape(quarter_couplings, quarters, row_coun...  15.5 us
    ppermute x7, waiting for transfers between devices, per_device(): lax.ppermute(val, 'pairs', [(ii, ii ^ b) for ii in range(inter)])  14.9 us
    unnamed x20, local copies, waits for them, and re-layouts  6.77 us
    all_to_all x1, starting transfers between devices, per_device(): lax.all_to_all(coupled_term.reshape(quarter_couplings, quarters, row_coun...  3.67 us
    dot_general x1, matrix products, per_device(): jnp.einsum('pc,crd->prd', target_select, scattered, preferred_element_typ...  1.98 us
    gather x1, local copies, waits for them, and re-layouts, per_device(): jnp.take(sent, picked.reshape(-1), axis=0)  1.87 us
  transfers between devices with their start and end apart: 8, of which 4 were waited for; matrix products, arithmetic and copies ran while one was open for 5% of the time, Pallas kernels for 0%

profile of v1, /device:TPU:0, one launch (start us, length us, event | category | flops | bytes accessed | tf_op | source)
XLA Modules:
  0.0 90.2 jit_solution(15913262224274623537)
XLA Ops:
  0.7 1.4 %select_reduce_fusion.1 = (s32[128]{0:T(128)}, s32[128]{0:T(128)S(1)}) fusion(s32[64]{0:T(128)} %param.13, s32[128]{0:T(128)} %param.15, s32[128]{0:T(128)} %param.14), kind=kLoop, calls=%fused_computation.34 | loop fusion | flops 48896 | bytes 2304 | tf_op jit(solution)/shard_map/reduce_sum | solution.py:27
  3.6 1.9 %gather_fusion = bf16[16,96,384]{2,1,0:T(8,128)(2,1)S(1)} fusion(bf16[8,96,384]{2,1,0:T(8,128)(2,1)} %param.9, s32[1024]{0:T(1024)S(1)} %get-tuple-element.29), kind=kCustom, calls=%fused_computation | custom fusion | bytes 2359360 | tf_op jit(solution)/shard_map/jit(_take)/gather | solution.py:80
  5.9 6.1 %collective-permute-start.6 = (bf16[1,2,96,384]{3,2,1,0:T(8,128)(2,1)S(1)}, bf16[1,2,96,384]{3,2,1,0:T(8,128)(2,1)S(1)}, u32[]{:S(2)}, u32[]{:S(2)}) collective-permute-start(bf16[1,2,96,384]{3,2,1,0:T(8,128)(2,1)S(1)} %get-tuple-element.16), channel_id=1, source_target_pairs={{0,28},{4,24},{8,20},{12,16},{16,12},{20,8},{24,4},{28,0},{1,29},{... | collective-permute-start | bytes 442376 | tf_op jit(solution)/shard_map/ppermute | solution.py:90
  12.9 2.0 %collective-permute-start.3 = (bf16[1,2,96,384]{3,2,1,0:T(8,128)(2,1)S(1)}, bf16[1,2,96,384]{3,2,1,0:T(8,128)(2,1)}, u32[]{:S(2)}, u32[]{:S(2)}) collective-permute-start(bf16[1,2,96,384]{3,2,1,0:T(8,128)(2,1)S(1)} %get-tuple-element.19), channel_id=1, source_target_pairs={{0,16},{4,20},{8,24},{12,28},{16,0},{20,4},{24,8},{28,12},{1,17},{... | collective-permute-start | bytes 442376 | tf_op jit(solution)/shard_map/ppermute | solution.py:90
  15.0 1.6 %collective-permute-start = (bf16[1,2,96,384]{3,2,1,0:T(8,128)(2,1)S(1)}, bf16[1,2,96,384]{3,2,1,0:T(8,128)(2,1)}, u32[]{:S(2)}, u32[]{:S(2)}) collective-permute-start(bf16[1,2,96,384]{3,2,1,0:T(8,128)(2,1)S(1)} %get-tuple-element.22), channel_id=1, source_target_pairs={{0,4},{4,0},{8,12},{12,8},{16,20},{20,16},{24,28},{28,24},{1,5},{5... | collective-permute-start | bytes 442376 | tf_op jit(solution)/shard_map/ppermute | solution.py:90
  16.8 3.4 %collective-permute-done = bf16[1,2,96,384]{3,2,1,0:T(8,128)(2,1)} collective-permute-done((bf16[1,2,96,384]{3,2,1,0:T(8,128)(2,1)S(1)}, bf16[1,2,96,384]{3,2,1,0:T(8,128)(2,1)}, u32[]{:S(2)}, u32[]{:S(2)}) %collective-permute-start) | collective-permute-done | bytes 147488 | tf_op jit(solution)/shard_map/ppermute | solution.py:90
  20.2 4.2 %collective-permute-start.1 = (bf16[1,2,96,384]{3,2,1,0:T(8,128)(2,1)S(1)}, bf16[1,2,96,384]{3,2,1,0:T(8,128)(2,1)S(1)}, u32[]{:S(2)}, u32[]{:S(2)}) collective-permute-start(bf16[1,2,96,384]{3,2,1,0:T(8,128)(2,1)S(1)} %get-tuple-element.21), channel_id=1, source_target_pairs={{0,8},{4,12},{8,0},{12,4},{16,24},{20,28},{24,16},{28,20},{1,9},{5... | collective-permute-start | bytes 442376 | tf_op jit(solution)/shard_map/ppermute | solution.py:90
  24.4 0.9 %bitcast_dynamic-update-slice_fusion.6 = bf16[8,1,2,96,384]{4,3,2,0,1:T(8,128)(2,1)S(1)} fusion(bf16[8,1,2,96,384]{4,3,2,0,1:T(8,128)(2,1)S(1)} %get-tuple-element.23, bf16[1,2,96,384]{3,2,1,0:T(8,128)(2,1)} %collective-permute-done), kind=kLoop, calls=%fused_computation.19 | loop fusion | bytes 294912
  25.3 2.5 %collective-permute-done.1 = bf16[1,2,96,384]{3,2,1,0:T(8,128)(2,1)S(1)} collective-permute-done((bf16[1,2,96,384]{3,2,1,0:T(8,128)(2,1)S(1)}, bf16[1,2,96,384]{3,2,1,0:T(8,128)(2,1)S(1)}, u32[]{:S(2)}, u32[]{:S(2)}) %collective-permute-start.1) | collective-permute-done | bytes 147488 | tf_op jit(solution)/shard_map/ppermute | solution.py:90
  27.8 2.7 %collective-permute-start.2 = (bf16[1,2,96,384]{3,2,1,0:T(8,128)(2,1)S(1)}, bf16[1,2,96,384]{3,2,1,0:T(8,128)(2,1)S(1)}, u32[]{:S(2)}, u32[]{:S(2)}) collective-permute-start(bf16[1,2,96,384]{3,2,1,0:T(8,128)(2,1)S(1)} %get-tuple-element.20), channel_id=1, source_target_pairs={{0,12},{4,8},{8,4},{12,0},{16,28},{20,24},{24,20},{28,16},{1,13},{... | collective-permute-start | bytes 442376 | tf_op jit(solution)/shard_map/ppermute | solution.py:90
  30.4 9.0 %collective-permute-done.2 = bf16[1,2,96,384]{3,2,1,0:T(8,128)(2,1)S(1)} collective-permute-done((bf16[1,2,96,384]{3,2,1,0:T(8,128)(2,1)S(1)}, bf16[1,2,96,384]{3,2,1,0:T(8,128)(2,1)S(1)}, u32[]{:S(2)}, u32[]{:S(2)}) %collective-permute-start.2) | collective-permute-done | bytes 147488 | tf_op jit(solution)/shard_map/ppermute | solution.py:90
  39.5 0.9 %bitcast_dynamic-update-slice_fusion.3 = bf16[8,1,2,96,384]{4,3,2,0,1:T(8,128)(2,1)S(1)} fusion(bf16[8,1,2,96,384]{4,3,2,0,1:T(8,128)(2,1)S(1)} %bitcast_dynamic-update-slice_fusion.4, bf16[1,2,96,384]{3,2,1,0:T(8,128)(2,1)} %collective-permute-done.3), kind=kLoop, calls=%fused_computation.16 | loop fusion | bytes 294912
  40.4 0.9 %bitcast_dynamic-update-slice_fusion.2 = bf16[8,1,2,96,384]{4,3,2,0,1:T(8,128)(2,1)S(1)} fusion(bf16[8,1,2,96,384]{4,3,2,0,1:T(8,128)(2,1)S(1)} %bitcast_dynamic-update-slice_fusion.3, bf16[1,2,96,384]{3,2,1,0:T(8,128)(2,1)} %collective-permute-done.4), kind=kLoop, calls=%fused_computation.15 | loop fusion | bytes 294912
  41.4 0.9 %bitcast_dynamic-update-slice_fusion.1 = bf16[8,1,2,96,384]{4,3,2,0,1:T(8,128)(2,1)S(1)} fusion(bf16[8,1,2,96,384]{4,3,2,0,1:T(8,128)(2,1)S(1)} %bitcast_dynamic-update-slice_fusion.2, bf16[1,2,96,384]{3,2,1,0:T(8,128)(2,1)} %collective-permute-done.5), kind=kLoop, calls=%fused_computation.14 | loop fusion | bytes 294912
  42.4 0.8 gather_fusion.1
  43.2 0.8 gather_fusion.2
  44.2 18.4 %all_to_all.30 = bf16[4,4,96,384]{3,2,1,0:T(8,128)(2,1)S(1)} all-to-all(bf16[4,4,96,384]{3,2,1,0:T(8,128)(2,1)S(1)} %broadcast_select_fusion.1), channel_id=1, replica_groups=mesh['pairs'=8,'dom'=4] {'dom'}, dimensions={0} | all-to-all | bytes 2359296 | tf_op jit(solution)/shard_map/all_to_all | solution.py:95
  63.3 1.8 %multiply_convert_fusion = bf16[4,384,384]{2,1,0:T(8,128)(2,1)S(1)} fusion(bf16[4,384,384]{2,1,0:T(8,128)(2,1)S(1)} %copy-done, bf16[4,384,384]{2,1,0:T(8,128)(2,1)S(1)} %bitcast.74, f32[4]{0:T(128)S(1)} %copy-done.4), kind=kOutput, calls=%fused_computation.3 | convolution fusion | flops 907739136 | bytes 3538960 | tf_op jit(solution)/shard_map/cad,ced->cae/dot_general | solution.py:101
  65.1 1.2 %copy.51 = bf16[4,4,96,384]{3,2,0,1:T(8,128)(2,1)} copy(bf16[4,4,96,384]{3,2,1,0:T(8,128)(2,1)S(1)} %bitcast.75) | data formatting | bytes 2359296 | tf_op jit(solution)/shard_map/reshape | solution.py:106
  66.2 3.7 %all-to-all-start.1 = ((bf16[4,4,96,384]{3,2,0,1:T(8,128)(2,1)}), bf16[4,4,96,384]{3,2,0,1:T(8,128)(2,1)S(1)}, u32[]{:S(2)}, u32[]{:S(2)}) async-start(bf16[4,4,96,384]{3,2,0,1:T(8,128)(2,1)} %copy.51), calls=%async_computation.1 | async-start | bytes 2359296 | tf_op jit(solution)/shard_map/all_to_all | solution.py:105
  70.2 15.5 %all-to-all-done.1 = bf16[4,4,96,384]{3,2,0,1:T(8,128)(2,1)S(1)} async-done(((bf16[4,4,96,384]{3,2,0,1:T(8,128)(2,1)}), bf16[4,4,96,384]{3,2,0,1:T(8,128)(2,1)S(1)}, u32[]{:S(2)}, u32[]{:S(2)}) %all-to-all-start.1) | async-done | bytes 1179680 | tf_op jit(solution)/shard_map/all_to_all | solution.py:105
  85.7 2.0 %convert_subtract_fusion = (f32[8,96,384]{2,0,1:T(8,128)S(1)}, f32[8,96,384]{2,0,1:T(8,128)S(1)}) fusion(f32[8]{0:T(128)S(1)} %copy-done.5, f32[8,384]{1,0:T(8,128)S(1)} %copy-done.3, f32[8,96]{0,1:T(8,128)S(1)} %copy.45, bf16[8,96,384]{2,1,0:T(8,128)(2,1)S(1)} %copy-done.1, bf16[16,96,384]{2,1,0:T(8,128)(2,1)S(1)} %bitcast.73, s32[16]{0:T(128)S(1)} %fusion.11, ...), kind=kOutput, calls=%fused_computation.5 | convolution fusion | flops 12091520 | bytes 4734048 | tf_op jit(solution)/shard_map/pc,crd->prd/dot_general | solution.py:112
  87.7 1.2 %copy.53 = f32[8,96,384]{2,1,0:T(8,128)} copy(f32[8,96,384]{2,0,1:T(8,128)S(1)} %get-tuple-element.26) | data formatting | bytes 2359296
  88.9 1.2 %copy.54 = f32[8,96,384]{2,1,0:T(8,128)} copy(f32[8,96,384]{2,0,1:T(8,128)S(1)} %get-tuple-element.27) | data formatting | bytes 2359296
  (58 shorter events, 4.2 us)
Async XLA Ops:
  0.6 62.1 %copy-start = (bf16[4,384,384]{2,1,0:T(8,128)(2,1)S(1)}, bf16[4,384,384]{2,1,0:T(8,128)(2,1)}, u32[]{:S(2)}) copy-start(bf16[4,384,384]{2,1,0:T(8,128)(2,1)} %param.17) | copy-start | bytes 3538948
  5.9 36.5 %collective-permute-start.6 = (bf16[1,2,96,384]{3,2,1,0:T(8,128)(2,1)S(1)}, bf16[1,2,96,384]{3,2,1,0:T(8,128)(2,1)S(1)}, u32[]{:S(2)}, u32[]{:S(2)}) collective-permute-start(bf16[1,2,96,384]{3,2,1,0:T(8,128)(2,1)S(1)} %get-tuple-element.16), channel_id=1, source_target_pairs={{0,28},{4,24},{8,20},{12,16},{16,12},{20,8},{24,4},{28,0},{1,29},{... | collective-permute-start | bytes 442376 | tf_op jit(solution)/shard_map/ppermute | solution.py:90
  12.0 29.4 %collective-permute-start.5 = (bf16[1,2,96,384]{3,2,1,0:T(8,128)(2,1)S(1)}, bf16[1,2,96,384]{3,2,1,0:T(8,128)(2,1)}, u32[]{:S(2)}, u32[]{:S(2)}) collective-permute-start(bf16[1,2,96,384]{3,2,1,0:T(8,128)(2,1)S(1)} %get-tuple-element.17), channel_id=1, source_target_pairs={{0,24},{4,28},{8,16},{12,20},{16,8},{20,12},{24,0},{28,4},{1,25},{... | collective-permute-start | bytes 442376 | tf_op jit(solution)/shard_map/ppermute | solution.py:90
  12.2 28.3 %collective-permute-start.4 = (bf16[1,2,96,384]{3,2,1,0:T(8,128)(2,1)S(1)}, bf16[1,2,96,384]{3,2,1,0:T(8,128)(2,1)}, u32[]{:S(2)}, u32[]{:S(2)}) collective-permute-start(bf16[1,2,96,384]{3,2,1,0:T(8,128)(2,1)S(1)} %get-tuple-element.18), channel_id=1, source_target_pairs={{0,20},{4,16},{8,28},{12,24},{16,4},{20,0},{24,12},{28,8},{1,21},{... | collective-permute-start | bytes 442376 | tf_op jit(solution)/shard_map/ppermute | solution.py:90
  12.9 26.6 %collective-permute-start.3 = (bf16[1,2,96,384]{3,2,1,0:T(8,128)(2,1)S(1)}, bf16[1,2,96,384]{3,2,1,0:T(8,128)(2,1)}, u32[]{:S(2)}, u32[]{:S(2)}) collective-permute-start(bf16[1,2,96,384]{3,2,1,0:T(8,128)(2,1)S(1)} %get-tuple-element.19), channel_id=1, source_target_pairs={{0,16},{4,20},{8,24},{12,28},{16,0},{20,4},{24,8},{28,12},{1,17},{... | collective-permute-start | bytes 442376 | tf_op jit(solution)/shard_map/ppermute | solution.py:90
  15.0 5.2 %collective-permute-start = (bf16[1,2,96,384]{3,2,1,0:T(8,128)(2,1)S(1)}, bf16[1,2,96,384]{3,2,1,0:T(8,128)(2,1)}, u32[]{:S(2)}, u32[]{:S(2)}) collective-permute-start(bf16[1,2,96,384]{3,2,1,0:T(8,128)(2,1)S(1)} %get-tuple-element.22), channel_id=1, source_target_pairs={{0,4},{4,0},{8,12},{12,8},{16,20},{20,16},{24,28},{28,24},{1,5},{5... | collective-permute-start | bytes 442376 | tf_op jit(solution)/shard_map/ppermute | solution.py:90
  20.2 7.5 %collective-permute-start.1 = (bf16[1,2,96,384]{3,2,1,0:T(8,128)(2,1)S(1)}, bf16[1,2,96,384]{3,2,1,0:T(8,128)(2,1)S(1)}, u32[]{:S(2)}, u32[]{:S(2)}) collective-permute-start(bf16[1,2,96,384]{3,2,1,0:T(8,128)(2,1)S(1)} %get-tuple-element.21), channel_id=1, source_target_pairs={{0,8},{4,12},{8,0},{12,4},{16,24},{20,28},{24,16},{28,20},{1,9},{5... | collective-permute-start | bytes 442376 | tf_op jit(solution)/shard_map/ppermute | solution.py:90
  27.8 11.7 %collective-permute-start.2 = (bf16[1,2,96,384]{3,2,1,0:T(8,128)(2,1)S(1)}, bf16[1,2,96,384]{3,2,1,0:T(8,128)(2,1)S(1)}, u32[]{:S(2)}, u32[]{:S(2)}) collective-permute-start(bf16[1,2,96,384]{3,2,1,0:T(8,128)(2,1)S(1)} %get-tuple-element.20), channel_id=1, source_target_pairs={{0,12},{4,8},{8,4},{12,0},{16,28},{20,24},{24,20},{28,16},{1,13},{... | collective-permute-start | bytes 442376 | tf_op jit(solution)/shard_map/ppermute | solution.py:90
  62.6 0.7 copy-start.4
  66.2 3.7 %copy-start.2 = (s32[128]{0:T(128)S(1)}, s32[128]{0:T(128)}, u32[]{:S(2)}) copy-start(s32[128]{0:T(128)} %get-tuple-element.12) | copy-start | bytes 1540
  66.2 3.8 %copy-start.3 = (f32[8,384]{1,0:T(8,128)S(1)}, f32[8,384]{1,0:T(8,128)}, u32[]{:S(2)}) copy-start(f32[8,384]{1,0:T(8,128)} %param.11) | copy-start | bytes 36868
  66.2 19.5 %copy-start.1 = (bf16[8,96,384]{2,1,0:T(8,128)(2,1)S(1)}, bf16[8,96,384]{2,1,0:T(8,128)(2,1)}, u32[]{:S(2)}) copy-start(bf16[8,96,384]{2,1,0:T(8,128)(2,1)} %param.9) | copy-start | bytes 1769476
  66.2 19.5 %copy-start.5 = (f32[8]{0:T(128)S(1)}, f32[8]{0:T(128)}, u32[]{:S(2)}) copy-start(f32[8]{0:T(128)} %param.12) | copy-start | bytes 100
  66.2 19.5 %all-to-all-start.1 = ((bf16[4,4,96,384]{3,2,0,1:T(8,128)(2,1)}), bf16[4,4,96,384]{3,2,0,1:T(8,128)(2,1)S(1)}, u32[]{:S(2)}, u32[]{:S(2)}) async-start(bf16[4,4,96,384]{3,2,0,1:T(8,128)(2,1)} %copy.51), calls=%async_computation.1 | async-start | bytes 2359296 | tf_op jit(solution)/shard_map/all_to_all | solution.py:105
